TPU v7x, 32 devices: a whole 2x2x4 slice. The times are simulated.
32 devices in a mesh: row: 8 (over y, x, core), col: 4 (over z).
Axes of the slice: x: 2, y: 2, z: 4, core: 2. Of those that a mesh axis runs over, the one named last changes fastest.
Arguments:
- mode_block: float32 [32768, 256], P(('row', 'col')), may hold values from -80 to 80
- k_blocks: float32 [256, 3, 128, 128], P(('row', 'col')), may hold values from -1 to 9
- block_cols: int32 [256, 3], P(('row', 'col')), may hold values from 0 to 255, as said below
- panel_node: int32 [4096], replicated, may hold values from 0 to 32767, as said below
- added_mass: bfloat16 [4096, 4096], P('row', 'col'), may hold values from -0.125 to 0.125
- low_edge: int32 [256], replicated, may hold values from 4 to 8
- high_edge: int32 [256], replicated, may hold values from 40 to 56
Outputs:
- filtered: float32 [32768, 256], P(('row', 'col'))
Inputs may be any that keep to these rules, and one draw needn't show every extreme that they name: `panel_node`: distinct shell rows. Cut the panels into 32 aligned blocks of 128; in each block at most 8 panels lie on the 1024 rows of one shell device (rows d * 1024 to (d + 1) * 1024 - 1), exactly 8 for some device, and the panels of a block on one device are consecutive. `block_cols`: row i holds i first, then two different block rows among i - 2 to i + 2 other than i.
All inputs are finite; a program needn't handle non-finite values.
Results may differ from a plain program's by a relative error of at most 0.0015.
Values may be sent and summed in bfloat16 or wider, within the bound.
A program may use at most 64 MiB of HBM per device.

v0:
```python
import jax
import jax.numpy as jnp
from jax import lax
from jax.sharding import PartitionSpec as P

DEGREE = 3
OUTER = 2


def with_halo(block, sides, width):
    for axis, dim in sides:
        count = lax.axis_size(axis)
        forward = [(i, i + 1) for i in range(count - 1)]
        backward = [(target, source) for source, target in forward]
        low = lax.ppermute(
            lax.slice_in_dim(block, block.shape[dim] - width, None, axis=dim), axis, forward
        )
        high = lax.ppermute(lax.slice_in_dim(block, 0, width, axis=dim), axis, backward)
        block = jnp.concatenate([low, block, high], axis=dim)
    return block


def body(mode_block, k_blocks, block_cols, panel_node, added_mass, low_edge, high_edge):
    n_row = lax.axis_size("row")
    n_col = lax.axis_size("col")
    devices = n_row * n_col
    my_row = lax.axis_index("row")
    my_col = lax.axis_index("col")
    linear = my_row * n_col + my_col
    rows_dev = mode_block.shape[0]
    mode_width = mode_block.shape[1]
    block_size = k_blocks.shape[2]
    blocks_dev = rows_dev // block_size
    panel_count = panel_node.shape[0]
    per_block = panel_count // devices
    slot_count = 2 * ((per_block + devices - 1) // devices)
    flat_total = devices * slot_count
    panel_rows = panel_node.reshape(devices, per_block)
    source = panel_rows // rows_dev
    within = jnp.arange(per_block)
    earlier = within[None, :] < within[:, None]
    same_source = source[:, :, None] == source[:, None, :]
    slot_rank = jnp.sum((same_source & earlier[None, :, :]).astype(jnp.int32), axis=2)
    block_ids = jnp.arange(devices)[:, None]
    target = block_ids % n_row * n_col + block_ids // n_row
    owned = source == linear
    local_row = panel_rows - linear * rows_dev
    send_flat = jnp.where(owned, target * slot_count + slot_rank, flat_total)
    send_index = jnp.full((flat_total,), rows_dev, dtype=jnp.int32)
    send_index = send_index.at[send_flat.reshape(-1)].set(local_row.reshape(-1), mode="drop")
    return_rows = jnp.where(owned, local_row, rows_dev)
    return_index = jnp.full((rows_dev,), flat_total, dtype=jnp.int32)
    return_index = return_index.at[return_rows.reshape(-1)].set(
        (block_ids * slot_count + slot_rank).reshape(-1), mode="drop"
    )
    in_block = my_col * n_row + my_row
    in_source = lax.dynamic_index_in_dim(source, in_block, 0, keepdims=False)
    in_slot = lax.dynamic_index_in_dim(slot_rank, in_block, 0, keepdims=False)
    in_flat = in_source * slot_count + in_slot
    out_source = lax.dynamic_index_in_dim(source, linear, 0, keepdims=False)
    out_slot = lax.dynamic_index_in_dim(slot_rank, linear, 0, keepdims=False)
    out_index = jnp.full((flat_total,), per_block, dtype=jnp.int32)
    out_index = out_index.at[out_source * slot_count + out_slot].set(within)
    row_source = lax.dynamic_slice_in_dim(source, my_row * n_col, n_col, 0)
    row_slot = lax.dynamic_slice_in_dim(slot_rank, my_row * n_col, n_col, 0)
    row_flat = (
        row_source * (n_col * slot_count) + jnp.arange(n_col)[:, None] * slot_count + row_slot
    )
    part_index = jnp.full((devices * n_col * slot_count,), n_col * per_block, dtype=jnp.int32)
    part_index = part_index.at[row_flat.reshape(-1)].set(jnp.arange(n_col * per_block))
    local_cols = block_cols - (linear * blocks_dev - 2)
    zero_bf = jnp.zeros((1, mode_width), jnp.bfloat16)
    zero_row = jnp.zeros((1, mode_width), jnp.float32)

    def stiffness(vectors):
        padded = with_halo(vectors, ((("row", "col"), 0),), 2 * block_size)
        pieces = padded.reshape(blocks_dev + 4, block_size, mode_width)
        chosen = pieces[local_cols]
        product = jnp.einsum("rkij,rkjn->rin", k_blocks, chosen, precision=lax.Precision.HIGHEST)
        return product.reshape(rows_dev, mode_width)

    def accumulate(arrived_piece):
        return jnp.dot(added_mass, arrived_piece, preferred_element_type=jnp.float32)

    def fluid_loads(vectors):
        rounded = jnp.concatenate([vectors.astype(jnp.bfloat16), zero_bf], axis=0)
        outgoing = rounded[send_index]
        arrived = lax.all_to_all(
            outgoing.reshape(devices, slot_count, mode_width),
            ("row", "col"),
            split_axis=0,
            concat_axis=0,
            tiled=True,
        )
        arrived = arrived.reshape(flat_total, mode_width)
        wetted = arrived[in_flat]
        partial_value = accumulate(lax.all_gather(wetted, "row", axis=0, tiled=True))
        pressure = lax.psum_scatter(partial_value, "col", scatter_dimension=0, tiled=True)
        padded_press = jnp.concatenate([pressure, zero_row], axis=0)
        sending = padded_press[out_index].reshape(devices, slot_count, mode_width)
        summed = lax.all_to_all(
            sending, ("row", "col"), split_axis=0, concat_axis=0, tiled=True
        ).reshape(flat_total, mode_width)
        padded_sum = jnp.concatenate([summed, zero_row], axis=0)
        return padded_sum[return_index]

    def operate(vectors):
        return stiffness(vectors) + fluid_loads(vectors)

    lower = low_edge.astype(jnp.float32) * 0.25
    upper = high_edge.astype(jnp.float32) * 0.25
    centre = 0.5 * (upper + lower)
    radius = 0.5 * (upper - lower)
    total_rows = rows_dev * devices
    current = mode_block
    for outer_no in range(OUTER):
        previous = current
        current = (operate(current) - centre * current) / radius
        for degree_no in range(DEGREE - 1):
            following = 2.0 * (operate(current) - centre * current) / radius - previous
            previous = current
            current = following
        squares = lax.psum(jnp.sum(current * current, axis=0), ("row", "col"))
        current = current / jnp.sqrt(squares / total_rows + 1e-06)
    return current


def solution(mesh):
    placed = (
        P(("row", "col"), None),
        P(("row", "col"), None, None, None),
        P(("row", "col"), None),
        P(),
        P("row", "col"),
        P(),
        P(),
    )
    return jax.shard_map(
        body, mesh=mesh, in_specs=placed, out_specs=P(("row", "col"), None), check_vma=False
    )
```

profile of v0, /device:TPU:0, one launch (start us, length us, event | category | flops | bytes accessed | tf_op | source)
XLA Modules:
  0.0 587.2 jit_solution(11731140511086322295)
XLA Ops:
  9.5 15.5 %scatter_custom_fusion = s32[256]{0:T(256)S(1)} fusion(s32[4096]{0:T(1024)S(1)} %get-tuple-element.35, s32[4096]{0:T(1024)S(1)} %get-tuple-element.20, s32[]{:T(128)} %constant.94.clone.1), kind=kCustom, calls=%fused_computation.139 | custom fusion | bytes 1028 | tf_op jit(solution)/shard_map/scatter | solution.py:50
  28.2 7.3 %all-to-all-start = ((bf16[32,8,256]{2,1,0:T(8,128)(2,1)}), bf16[32,8,256]{2,1,0:T(8,128)(2,1)S(1)}, u32[]{:S(2)}, u32[]{:S(2)}) async-start(bf16[32,8,256]{2,1,0:T(8,128)(2,1)} %bitcast.8), calls=%async_computation | async-start | bytes 262144 | tf_op jit(solution)/shard_map/all_to_all | solution.py:88
  44.8 13.9 %all-gather = bf16[1024,256]{1,0:T(8,128)(2,1)S(1)} all-gather(bf16[128,256]{1,0:T(8,128)(2,1)S(1)} %gather_fusion.2), channel_id=2, replica_groups=mesh['row'=8,'col'=4] {'row'}, dimensions={0}, use_global_device_ids=true | all-gather | bytes 589824 | tf_op jit(solution)/shard_map/all_gather | solution.py:97
  60.3 15.5 %scatter_custom_fusion.2 = s32[1024]{0:T(1024)S(1)} fusion(s32[4096]{0:T(1024)S(1)} %get-tuple-element.19, s32[4096]{0:T(1024)S(1)} %add_bitcast_fusion, s32[]{:T(128)} %constant.101.clone.1), kind=kCustom, calls=%fused_computation.110 | custom fusion | bytes 4100 | tf_op jit(solution)/shard_map/scatter | solution.py:53
  91.9 5.1 fusion.59
  106.0 14.0 %all_to_all.60 = bf16[32,8,256]{2,1,0:T(8,128)(2,1)S(1)} all-to-all(bf16[32,8,256]{2,1,0:T(8,128)(2,1)S(1)} %bitcast.215), channel_id=1, replica_groups=mesh['row'=8,'col'=4] {'row','col'}, dimensions={0} | all-to-all | bytes 262144 | tf_op jit(solution)/shard_map/all_to_all | solution.py:88
  120.8 9.6 %all-gather.1 = bf16[1024,256]{1,0:T(8,128)(2,1)S(1)} all-gather(bf16[128,256]{1,0:T(8,128)(2,1)S(1)} %gather_fusion.7), channel_id=3, replica_groups=mesh['row'=8,'col'=4] {'row'}, dimensions={0}, use_global_device_ids=true | all-gather | bytes 589824 | tf_op jit(solution)/shard_map/all_gather | solution.py:97
  136.7 20.1 %reduce-scatter.9.cloned.1.call-done = f32[128,256]{0,1:T(8,128)} async-done(((f32[512,256]{0,1:T(8,128)}), f32[128,256]{0,1:T(8,128)}) %reduce-scatter.9.cloned.1.call-update) | async-done | bytes 131088 | tf_op jit(solution)/shard_map/reduce_scatter | solution.py:98
  170.6 5.1 fusion.60
  175.8 4.7 gather_fusion.9
  185.1 14.0 %all_to_all.61 = bf16[32,8,256]{2,1,0:T(8,128)(2,1)S(1)} all-to-all(bf16[32,8,256]{2,1,0:T(8,128)(2,1)S(1)} %bitcast.216), channel_id=1, replica_groups=mesh['row'=8,'col'=4] {'row','col'}, dimensions={0} | all-to-all | bytes 262144 | tf_op jit(solution)/shard_map/all_to_all | solution.py:88
  200.0 9.1 %all-gather.2 = bf16[1024,256]{1,0:T(8,128)(2,1)S(1)} all-gather(bf16[128,256]{1,0:T(8,128)(2,1)S(1)} %gather_fusion.12), channel_id=4, replica_groups=mesh['row'=8,'col'=4] {'row'}, dimensions={0}, use_global_device_ids=true | all-gather | bytes 589824 | tf_op jit(solution)/shard_map/all_gather | solution.py:97
  215.4 20.1 %reduce-scatter.11.cloned.1.call-done = f32[128,256]{0,1:T(8,128)} async-done(((f32[512,256]{0,1:T(8,128)}), f32[128,256]{0,1:T(8,128)}) %reduce-scatter.11.cloned.1.call-update) | async-done | bytes 131088 | tf_op jit(solution)/shard_map/reduce_scatter | solution.py:98
  249.4 5.1 fusion.61
  254.6 4.7 gather_fusion.14
  262.7 40.4 %psum.14 = f32[256]{0:T(256)S(1)} all-reduce(f32[256]{0:T(256)S(1)} %get-tuple-element.13), channel_id=1, replica_groups=mesh['row'=8,'col'=4] {'row','col'}, use_global_device_ids=true, to_apply=%region_8.9 | all-reduce | flops 256 | bytes 2048 | tf_op jit(solution)/shard_map/psum | solution.py:123
  306.6 12.7 %all_to_all.62 = bf16[32,8,256]{2,1,0:T(8,128)(2,1)S(1)} all-to-all(bf16[32,8,256]{2,1,0:T(8,128)(2,1)S(1)} %bitcast.217), channel_id=1, replica_groups=mesh['row'=8,'col'=4] {'row','col'}, dimensions={0} | all-to-all | bytes 262144 | tf_op jit(solution)/shard_map/all_to_all | solution.py:88
  320.1 9.1 %all-gather.3 = bf16[1024,256]{1,0:T(8,128)(2,1)S(1)} all-gather(bf16[128,256]{1,0:T(8,128)(2,1)S(1)} %gather_fusion.17), channel_id=5, replica_groups=mesh['row'=8,'col'=4] {'row'}, dimensions={0}, use_global_device_ids=true | all-gather | bytes 589824 | tf_op jit(solution)/shard_map/all_gather | solution.py:97
  335.5 20.1 %reduce-scatter.13.cloned.1.call-done = f32[128,256]{0,1:T(8,128)} async-done(((f32[512,256]{0,1:T(8,128)}), f32[128,256]{0,1:T(8,128)}) %reduce-scatter.13.cloned.1.call-update) | async-done | bytes 131088 | tf_op jit(solution)/shard_map/reduce_scatter | solution.py:98
  369.4 5.1 fusion.62
  374.5 4.7 gather_fusion.19
  383.5 14.0 %all_to_all.63 = bf16[32,8,256]{2,1,0:T(8,128)(2,1)S(1)} all-to-all(bf16[32,8,256]{2,1,0:T(8,128)(2,1)S(1)} %bitcast.218), channel_id=1, replica_groups=mesh['row'=8,'col'=4] {'row','col'}, dimensions={0} | all-to-all | bytes 262144 | tf_op jit(solution)/shard_map/all_to_all | solution.py:88
  398.4 9.3 %all-gather.4 = bf16[1024,256]{1,0:T(8,128)(2,1)S(1)} all-gather(bf16[128,256]{1,0:T(8,128)(2,1)S(1)} %gather_fusion.22), channel_id=6, replica_groups=mesh['row'=8,'col'=4] {'row'}, dimensions={0}, use_global_device_ids=true | all-gather | bytes 589824 | tf_op jit(solution)/shard_map/all_gather | solution.py:97
  414.0 20.1 %reduce-scatter.15.cloned.1.call-done = f32[128,256]{0,1:T(8,128)} async-done(((f32[512,256]{0,1:T(8,128)}), f32[128,256]{0,1:T(8,128)}) %reduce-scatter.15.cloned.1.call-update) | async-done | bytes 131088 | tf_op jit(solution)/shard_map/reduce_scatter | solution.py:98
  447.8 5.1 fusion.63
  453.0 4.7 gather_fusion.24
  462.3 14.0 %all_to_all.64 = bf16[32,8,256]{2,1,0:T(8,128)(2,1)S(1)} all-to-all(bf16[32,8,256]{2,1,0:T(8,128)(2,1)S(1)} %bitcast.214), channel_id=1, replica_groups=mesh['row'=8,'col'=4] {'row','col'}, dimensions={0} | all-to-all | bytes 262144 | tf_op jit(solution)/shard_map/all_to_all | solution.py:88
  477.2 9.1 %all-gather.5 = bf16[1024,256]{1,0:T(8,128)(2,1)S(1)} all-gather(bf16[128,256]{1,0:T(8,128)(2,1)S(1)} %gather_fusion.27), channel_id=7, replica_groups=mesh['row'=8,'col'=4] {'row'}, dimensions={0}, use_global_device_ids=true | all-gather | bytes 589824 | tf_op jit(solution)/shard_map/all_gather | solution.py:97
  491.8 21.1 %reduce-scatter.17.cloned.1.call-done = f32[128,256]{0,1:T(8,128)} async-done(((f32[512,256]{0,1:T(8,128)}), f32[128,256]{0,1:T(8,128)}) %reduce-scatter.17.cloned.1.call-update) | async-done | bytes 131088 | tf_op jit(solution)/shard_map/reduce_scatter | solution.py:98
  526.1 5.1 fusion.64
  531.3 4.7 gather_fusion.29
  538.5 40.5 %psum.15 = f32[256]{0:T(256)S(1)} all-reduce(f32[256]{0:T(256)S(1)} %get-tuple-element.5), channel_id=1, replica_groups=mesh['row'=8,'col'=4] {'row','col'}, use_global_device_ids=true, to_apply=%region_13.14 | all-reduce | flops 256 | bytes 2048 | tf_op jit(solution)/shard_map/psum | solution.py:123
  (159 shorter events, 168.8 us)
Async XLA Ops:
  6.5 85.4 %copy-start = (f32[8,3,128,128]{3,2,1,0:T(8,128)S(1)}, f32[8,3,128,128]{3,2,1,0:T(8,128)}, u32[]{:S(2)}) copy-start(f32[8,3,128,128]{3,2,1,0:T(8,128)} %param.8) | copy-start | bytes 4718596
  26.3 17.1 %copy-start.2 = (s32[8,3]{0,1:T(4,128)S(1)}, s32[8,3]{0,1:T(4,128)}, u32[]{:S(2)}) copy-start(s32[8,3]{0,1:T(4,128)} %param.9) | copy-start | bytes 292
  26.4 32.3 %copy-start.1 = (bf16[512,1024]{1,0:T(8,128)(2,1)S(1)}, bf16[512,1024]{1,0:T(8,128)(2,1)}, u32[]{:S(2)}) copy-start(bf16[512,1024]{1,0:T(8,128)(2,1)} %param.11) | copy-start | bytes 3145732
  28.2 15.7 %all-to-all-start = ((bf16[32,8,256]{2,1,0:T(8,128)(2,1)}), bf16[32,8,256]{2,1,0:T(8,128)(2,1)S(1)}, u32[]{:S(2)}, u32[]{:S(2)}) async-start(bf16[32,8,256]{2,1,0:T(8,128)(2,1)} %bitcast.8), calls=%async_computation | async-start | bytes 262144 | tf_op jit(solution)/shard_map/all_to_all | solution.py:88
  35.5 44.4 %reduce-scatter.7.cloned.1.call-start = ((), (), s32[]{:S(2)}) async-start(), calls=%async_computation.18 | async-start | bytes 655360 | tf_op jit(solution)/shard_map/reduce_scatter | solution.py:98
  37.4 48.1 %collective-permute-start = (f32[256,256]{1,0:T(8,128)}, f32[256,256]{1,0:T(8,128)S(1)}, u32[]{:S(2)}, u32[]{:S(2)}) collective-permute-start(f32[256,256]{1,0:T(8,128)} %get-tuple-element.31), channel_id=1, source_target_pairs={{0,1},{1,2},{2,3},{3,4},{4,5},{5,6},{6,7},{7,8},{8,9},{9,10},{10,1... | collective-permute-start | bytes 786440 | tf_op jit(solution)/shard_map/ppermute | solution.py:15
  41.1 44.4 %collective-permute-start.1 = (f32[256,256]{1,0:T(8,128)}, f32[256,256]{1,0:T(8,128)}, u32[]{:S(2)}, u32[]{:S(2)}) collective-permute-start(f32[256,256]{1,0:T(8,128)} %get-tuple-element.32), channel_id=1, source_target_pairs={{1,0},{2,1},{3,2},{4,3},{5,4},{6,5},{7,6},{8,7},{9,8},{10,9},{11,1... | collective-permute-start | bytes 786440 | tf_op jit(solution)/shard_map/ppermute | solution.py:18
  44.8 15.4 %copy-start.3 = (s32[256]{0:T(256)S(1)}, s32[256]{0:T(256)}, u32[]{:S(2)}) copy-start(s32[256]{0:T(256)} %param.13) | copy-start | bytes 3076
  44.8 15.4 %copy-start.4 = (s32[256]{0:T(256)S(1)}, s32[256]{0:T(256)}, u32[]{:S(2)}) copy-start(s32[256]{0:T(256)} %param.12) | copy-start | bytes 3076
  82.6 14.5 %all-to-all-start.1 = ((f32[32,8,256]{2,1,0:T(8,128)}), f32[32,8,256]{2,1,0:T(8,128)S(1)}, u32[]{:S(2)}, u32[]{:S(2)}) async-start(f32[32,8,256]{2,1,0:T(8,128)} %bitcast.15), calls=%async_computation.2 | async-start | bytes 524288 | tf_op jit(solution)/shard_map/all_to_all | solution.py:101
  85.5 71.3 %reduce-scatter.9.cloned.1.call-start = ((), (), s32[]{:S(2)}) async-start(), calls=%async_computation.19 | async-start | bytes 655360 | tf_op jit(solution)/shard_map/reduce_scatter | solution.py:98
  133.6 30.5 %collective-permute-start.2 = (f32[256,256]{1,0:T(8,128)}, f32[256,256]{1,0:T(8,128)S(1)}, u32[]{:S(2)}, u32[]{:S(2)}) collective-permute-start(f32[256,256]{1,0:T(8,128)} %get-tuple-element.29), channel_id=1, source_target_pairs={{0,1},{1,2},{2,3},{3,4},{4,5},{5,6},{6,7},{7,8},{8,9},{9,10},{10,1... | collective-permute-start | bytes 786440 | tf_op jit(solution)/shard_map/ppermute | solution.py:15
  135.4 28.8 %collective-permute-start.3 = (f32[256,256]{1,0:T(8,128)}, f32[256,256]{1,0:T(8,128)}, u32[]{:S(2)}, u32[]{:S(2)}) collective-permute-start(f32[256,256]{1,0:T(8,128)} %get-tuple-element.30), channel_id=1, source_target_pairs={{1,0},{2,1},{3,2},{4,3},{5,4},{6,5},{7,6},{8,7},{9,8},{10,9},{11,1... | collective-permute-start | bytes 786440 | tf_op jit(solution)/shard_map/ppermute | solution.py:18
  159.5 16.3 %all-to-all-start.3 = ((f32[32,8,256]{2,1,0:T(8,128)}), f32[32,8,256]{2,1,0:T(8,128)S(1)}, u32[]{:S(2)}, u32[]{:S(2)}) async-start(f32[32,8,256]{2,1,0:T(8,128)} %bitcast.27), calls=%async_computation.5 | async-start | bytes 524288 | tf_op jit(solution)/shard_map/all_to_all | solution.py:101
  164.1 71.3 %reduce-scatter.11.cloned.1.call-start = ((), (), s32[]{:S(2)}) async-start(), calls=%async_computation.20 | async-start | bytes 655360 | tf_op jit(solution)/shard_map/reduce_scatter | solution.py:98
  212.3 30.7 %collective-permute-start.4 = (f32[256,256]{1,0:T(8,128)}, f32[256,256]{1,0:T(8,128)S(1)}, u32[]{:S(2)}, u32[]{:S(2)}) collective-permute-start(f32[256,256]{1,0:T(8,128)} %get-tuple-element.27), channel_id=1, source_target_pairs={{0,1},{1,2},{2,3},{3,4},{4,5},{5,6},{6,7},{7,8},{8,9},{9,10},{10,1... | collective-permute-start | bytes 786440 | tf_op jit(solution)/shard_map/ppermute | solution.py:15
  214.1 28.9 %collective-permute-start.5 = (f32[256,256]{1,0:T(8,128)}, f32[256,256]{1,0:T(8,128)}, u32[]{:S(2)}, u32[]{:S(2)}) collective-permute-start(f32[256,256]{1,0:T(8,128)} %get-tuple-element.28), channel_id=1, source_target_pairs={{1,0},{2,1},{3,2},{4,3},{5,4},{6,5},{7,6},{8,7},{9,8},{10,9},{11,1... | collective-permute-start | bytes 786440 | tf_op jit(solution)/shard_map/ppermute | solution.py:18
  238.2 16.4 %all-to-all-start.5 = ((f32[32,8,256]{2,1,0:T(8,128)}), f32[32,8,256]{2,1,0:T(8,128)S(1)}, u32[]{:S(2)}, u32[]{:S(2)}) async-start(f32[32,8,256]{2,1,0:T(8,128)} %bitcast.38), calls=%async_computation.8 | async-start | bytes 524288 | tf_op jit(solution)/shard_map/all_to_all | solution.py:101
  242.8 112.8 %reduce-scatter.13.cloned.1.call-start = ((), (), s32[]{:S(2)}) async-start(), calls=%async_computation.21 | async-start | bytes 655360 | tf_op jit(solution)/shard_map/reduce_scatter | solution.py:98
  332.5 30.5 %collective-permute-start.6 = (f32[256,256]{1,0:T(8,128)}, f32[256,256]{1,0:T(8,128)S(1)}, u32[]{:S(2)}, u32[]{:S(2)}) collective-permute-start(f32[256,256]{1,0:T(8,128)} %get-tuple-element.25), channel_id=1, source_target_pairs={{0,1},{1,2},{2,3},{3,4},{4,5},{5,6},{6,7},{7,8},{8,9},{9,10},{10,1... | collective-permute-start | bytes 786440 | tf_op jit(solution)/shard_map/ppermute | solution.py:15
  334.2 28.8 %collective-permute-start.7 = (f32[256,256]{1,0:T(8,128)}, f32[256,256]{1,0:T(8,128)}, u32[]{:S(2)}, u32[]{:S(2)}) collective-permute-start(f32[256,256]{1,0:T(8,128)} %get-tuple-element.26), channel_id=1, source_target_pairs={{1,0},{2,1},{3,2},{4,3},{5,4},{6,5},{7,6},{8,7},{9,8},{10,9},{11,1... | collective-permute-start | bytes 786440 | tf_op jit(solution)/shard_map/ppermute | solution.py:18
  358.3 16.2 %all-to-all-start.7 = ((f32[32,8,256]{2,1,0:T(8,128)}), f32[32,8,256]{2,1,0:T(8,128)S(1)}, u32[]{:S(2)}, u32[]{:S(2)}) async-start(f32[32,8,256]{2,1,0:T(8,128)} %bitcast.49), calls=%async_computation.11 | async-start | bytes 524288 | tf_op jit(solution)/shard_map/all_to_all | solution.py:101
  362.9 71.1 %reduce-scatter.15.cloned.1.call-start = ((), (), s32[]{:S(2)}) async-start(), calls=%async_computation.22 | async-start | bytes 655360 | tf_op jit(solution)/shard_map/reduce_scatter | solution.py:98
  410.9 30.5 %collective-permute-start.8 = (f32[256,256]{1,0:T(8,128)}, f32[256,256]{1,0:T(8,128)S(1)}, u32[]{:S(2)}, u32[]{:S(2)}) collective-permute-start(f32[256,256]{1,0:T(8,128)} %get-tuple-element.23), channel_id=1, source_target_pairs={{0,1},{1,2},{2,3},{3,4},{4,5},{5,6},{6,7},{7,8},{8,9},{9,10},{10,1... | collective-permute-start | bytes 786440 | tf_op jit(solution)/shard_map/ppermute | solution.py:15
  412.7 28.7 %collective-permute-start.9 = (f32[256,256]{1,0:T(8,128)}, f32[256,256]{1,0:T(8,128)}, u32[]{:S(2)}, u32[]{:S(2)}) collective-permute-start(f32[256,256]{1,0:T(8,128)} %get-tuple-element.24), channel_id=1, source_target_pairs={{1,0},{2,1},{3,2},{4,3},{5,4},{6,5},{7,6},{8,7},{9,8},{10,9},{11,1... | collective-permute-start | bytes 786440 | tf_op jit(solution)/shard_map/ppermute | solution.py:18
  436.7 16.2 %all-to-all-start.9 = ((f32[32,8,256]{2,1,0:T(8,128)}), f32[32,8,256]{2,1,0:T(8,128)S(1)}, u32[]{:S(2)}, u32[]{:S(2)}) async-start(f32[32,8,256]{2,1,0:T(8,128)} %bitcast.60), calls=%async_computation.14 | async-start | bytes 524288 | tf_op jit(solution)/shard_map/all_to_all | solution.py:101
  441.4 71.5 %reduce-scatter.17.cloned.1.call-start = ((), (), s32[]{:S(2)}) async-start(), calls=%async_computation.23 | async-start | bytes 655360 | tf_op jit(solution)/shard_map/reduce_scatter | solution.py:98
  488.7 31.2 %collective-permute-start.10 = (f32[256,256]{1,0:T(8,128)S(1)}, f32[256,256]{1,0:T(8,128)S(1)}, u32[]{:S(2)}, u32[]{:S(2)}) collective-permute-start(f32[256,256]{1,0:T(8,128)S(1)} %get-tuple-element.21), channel_id=1, source_target_pairs={{0,1},{1,2},{2,3},{3,4},{4,5},{5,6},{6,7},{7,8},{8,9},{9,10},{10,1... | collective-permute-start | bytes 786440 | tf_op jit(solution)/shard_map/ppermute | solution.py:15
  490.5 29.4 %collective-permute-start.11 = (f32[256,256]{1,0:T(8,128)S(1)}, f32[256,256]{1,0:T(8,128)S(1)}, u32[]{:S(2)}, u32[]{:S(2)}) collective-permute-start(f32[256,256]{1,0:T(8,128)S(1)} %get-tuple-element.22), channel_id=1, source_target_pairs={{1,0},{2,1},{3,2},{4,3},{5,4},{6,5},{7,6},{8,7},{9,8},{10,9},{11,1... | collective-permute-start | bytes 786440 | tf_op jit(solution)/shard_map/ppermute | solution.py:18
  515.5 15.7 %all-to-all-start.11 = ((f32[32,8,256]{2,1,0:T(8,128)}), f32[32,8,256]{2,1,0:T(8,128)S(1)}, u32[]{:S(2)}, u32[]{:S(2)}) async-start(f32[32,8,256]{2,1,0:T(8,128)} %bitcast.71), calls=%async_computation.17 | async-start | bytes 524288 | tf_op jit(solution)/shard_map/all_to_all | solution.py:101
Sparse Core Ops, SparseCore 0:
  60.1 19.7 reduce-scatter.6
  131.9 24.8 reduce-scatter.8
  210.5 24.8 reduce-scatter.10
  330.7 24.8 reduce-scatter.12
  409.1 24.8 reduce-scatter.14
  487.7 25.0 reduce-scatter.16
where the time goes:
time: 597 us; the launch traced here: 587 us
  blocking collectives  210 us (35%)
  local copies, waits for them, and re-layouts  123 us (21%)
  waiting for transfers between devices  106 us (18%)
  starting transfers between devices  53.7 us (9%)
  other arithmetic  42.1 us (7%)
  matrix products  38.6 us (6%)
  between operations  14.5 us (2%)
    reduce_scatter x6, waiting for transfers between devices, fluid_loads(): lax.psum_scatter(partial_value, 'col', scatter_dimension=0, tiled=True)  105 us
    psum x2, blocking collectives, body(): squares = lax.psum(jnp.sum(current * current, axis=0), ('row', 'col'))  80.9 us
    all_to_all x5, blocking collectives, fluid_loads(): lax.all_to_all(outgoing.reshape(devices, slot_count, mode_width), ('row',...  68.7 us
    all_gather x6, blocking collectives, fluid_loads(): lax.all_gather(wetted, 'row', axis=0, tiled=True)  60.2 us
    dot_general x6, matrix products, stiffness(): jnp.einsum('rkij,rkjn->rin', k_blocks, chosen, precision=lax.Precision.HI...  30.9 us
    gather x6, local copies, waits for them, and re-layouts, fluid_loads(): return padded_sum[return_index]  28.2 us
    all_to_all x6, starting transfers between devices, fluid_loads(): lax.all_to_all(sending, ('row', 'col'), split_axis=0, concat_axis=0, tile...  25.7 us
    gather x6, local copies, waits for them, and re-layouts, stiffness(): chosen = pieces[local_cols]  22.7 us
  transfers between devices with their start and end apart: 25, of which 7 were waited for; matrix products, arithmetic and copies ran while one was open for 20% of the time, Pallas kernels for 0%

commit v1 on v0

--- a/solution.py
+++ b/solution.py
@@ -120,7 +120,11 @@
             following = 2.0 * (operate(current) - centre * current) / radius - previous
             previous = current
             current = following
-        squares = lax.psum(jnp.sum(current * current, axis=0), ("row", "col"))
+
+        def follow_weights_on(original):
+            return jax.lax.psum(jax.lax.psum(original, "col"), axis_name="row")
+
+        squares = follow_weights_on(jnp.sum(current * current, axis=0))
         current = current / jnp.sqrt(squares / total_rows + 1e-06)
     return current
 

time: 597 us -> 562 us (0.941)
  blocking collectives: 210 us -> 174 us
    psum x2 -> x4, blocking collectives: 80.9 us -> 47.9 us  [follow_weights_on(): return jax.lax.psum(jax.lax.psum(original, 'col'), axis_name='row')]
  transfers between devices with their start and end apart: 25 -> 25, of which waited for: 7 -> 7; matrix products, arithmetic and copies ran while one was open for 20% -> 21% of each run, Pallas kernels for 0% -> 0%
where the time goes in v1:
time: 562 us; the launch traced here: 551 us
  blocking collectives  174 us (31%)
  local copies, waits for them, and re-layouts  123 us (22%)
  waiting for transfers between devices  106 us (19%)
  starting transfers between devices  53.7 us (10%)
  other arithmetic  42 us (7%)
  matrix products  38.8 us (7%)
  between operations  14.4 us (3%)
    reduce_scatter x6, waiting for transfers between devices, fluid_loads(): lax.psum_scatter(partial_value, 'col', scatter_dimension=0, tiled=True)  105 us
    all_to_all x5, blocking collectives, fluid_loads(): lax.all_to_all(outgoing.reshape(devices, slot_count, mode_width), ('row',...  66.2 us
    all_gather x6, blocking collectives, fluid_loads(): lax.all_gather(wetted, 'row', axis=0, tiled=True)  60 us
    psum x4, blocking collectives, follow_weights_on(): return jax.lax.psum(jax.lax.psum(original, 'col'), axis_name='row')  47.9 us
    dot_general x6, matrix products, stiffness(): jnp.einsum('rkij,rkjn->rin', k_blocks, chosen, precision=lax.Precision.HI...  31.1 us
    gather x6, local copies, waits for them, and re-layouts, fluid_loads(): return padded_sum[return_index]  28.1 us
    all_to_all x6, starting transfers between devices, fluid_loads(): lax.all_to_all(sending, ('row', 'col'), split_axis=0, concat_axis=0, tile...  25.7 us
    gather x6, local copies, waits for them, and re-layouts, stiffness(): chosen = pieces[local_cols]  22.9 us
  transfers between devices with their start and end apart: 25, of which 7 were waited for; matrix products, arithmetic and copies ran while one was open for 21% of the time, Pallas kernels for 0%

profile of v1, /device:TPU:0, one launch (start us, length us, event | category | flops | bytes accessed | tf_op | source)
XLA Modules:
  0.0 551.4 jit_solution(9457661289626836668)
XLA Ops:
  9.5 15.5 %scatter_custom_fusion = s32[256]{0:T(256)S(1)} fusion(s32[4096]{0:T(1024)S(1)} %get-tuple-element.35, s32[4096]{0:T(1024)S(1)} %get-tuple-element.20, s32[]{:T(128)} %constant.94.clone.1), kind=kCustom, calls=%fused_computation.139 | custom fusion | bytes 1028 | tf_op jit(solution)/shard_map/scatter | solution.py:50
  28.2 7.3 %all-to-all-start = ((bf16[32,8,256]{2,1,0:T(8,128)(2,1)}), bf16[32,8,256]{2,1,0:T(8,128)(2,1)S(1)}, u32[]{:S(2)}, u32[]{:S(2)}) async-start(bf16[32,8,256]{2,1,0:T(8,128)(2,1)} %bitcast.8), calls=%async_computation | async-start | bytes 262144 | tf_op jit(solution)/shard_map/all_to_all | solution.py:88
  44.8 13.9 %all-gather = bf16[1024,256]{1,0:T(8,128)(2,1)S(1)} all-gather(bf16[128,256]{1,0:T(8,128)(2,1)S(1)} %gather_fusion.2), channel_id=2, replica_groups=mesh['row'=8,'col'=4] {'row'}, dimensions={0}, use_global_device_ids=true | all-gather | bytes 589824 | tf_op jit(solution)/shard_map/all_gather | solution.py:97
  60.3 15.5 %scatter_custom_fusion.2 = s32[1024]{0:T(1024)S(1)} fusion(s32[4096]{0:T(1024)S(1)} %get-tuple-element.19, s32[4096]{0:T(1024)S(1)} %add_bitcast_fusion, s32[]{:T(128)} %constant.101.clone.1), kind=kCustom, calls=%fused_computation.110 | custom fusion | bytes 4100 | tf_op jit(solution)/shard_map/scatter | solution.py:53
  92.0 5.2 fusion.59
  106.1 14.0 %all_to_all.60 = bf16[32,8,256]{2,1,0:T(8,128)(2,1)S(1)} all-to-all(bf16[32,8,256]{2,1,0:T(8,128)(2,1)S(1)} %bitcast.215), channel_id=1, replica_groups=mesh['row'=8,'col'=4] {'row','col'}, dimensions={0} | all-to-all | bytes 262144 | tf_op jit(solution)/shard_map/all_to_all | solution.py:88
  120.9 9.6 %all-gather.1 = bf16[1024,256]{1,0:T(8,128)(2,1)S(1)} all-gather(bf16[128,256]{1,0:T(8,128)(2,1)S(1)} %gather_fusion.7), channel_id=3, replica_groups=mesh['row'=8,'col'=4] {'row'}, dimensions={0}, use_global_device_ids=true | all-gather | bytes 589824 | tf_op jit(solution)/shard_map/all_gather | solution.py:97
  136.8 20.0 %reduce-scatter.9.cloned.1.call-done = f32[128,256]{0,1:T(8,128)} async-done(((f32[512,256]{0,1:T(8,128)}), f32[128,256]{0,1:T(8,128)}) %reduce-scatter.9.cloned.1.call-update) | async-done | bytes 131088 | tf_op jit(solution)/shard_map/reduce_scatter | solution.py:98
  159.5 4.7 all-to-all-start.3
  170.7 5.2 fusion.60
  185.2 14.0 %all_to_all.61 = bf16[32,8,256]{2,1,0:T(8,128)(2,1)S(1)} all-to-all(bf16[32,8,256]{2,1,0:T(8,128)(2,1)S(1)} %bitcast.216), channel_id=1, replica_groups=mesh['row'=8,'col'=4] {'row','col'}, dimensions={0} | all-to-all | bytes 262144 | tf_op jit(solution)/shard_map/all_to_all | solution.py:88
  200.1 9.1 %all-gather.2 = bf16[1024,256]{1,0:T(8,128)(2,1)S(1)} all-gather(bf16[128,256]{1,0:T(8,128)(2,1)S(1)} %gather_fusion.12), channel_id=4, replica_groups=mesh['row'=8,'col'=4] {'row'}, dimensions={0}, use_global_device_ids=true | all-gather | bytes 589824 | tf_op jit(solution)/shard_map/all_gather | solution.py:97
  215.4 20.1 %reduce-scatter.11.cloned.1.call-done = f32[128,256]{0,1:T(8,128)} async-done(((f32[512,256]{0,1:T(8,128)}), f32[128,256]{0,1:T(8,128)}) %reduce-scatter.11.cloned.1.call-update) | async-done | bytes 131088 | tf_op jit(solution)/shard_map/reduce_scatter | solution.py:98
  249.3 5.2 fusion.61
  262.6 12.1 %psum.28 = f32[256]{0:T(256)S(1)} all-reduce(f32[256]{0:T(256)S(1)} %get-tuple-element.13), channel_id=1, replica_groups=mesh['row'=8,'col'=4] {'col'}, use_global_device_ids=true, to_apply=%region_8.9 | all-reduce | flops 256 | bytes 2048 | tf_op jit(solution)/shard_map/psum | solution.py:125
  274.7 11.9 %psum.29 = f32[256]{0:T(256)S(1)} all-reduce(f32[256]{0:T(256)S(1)} %psum.28), channel_id=1, replica_groups=mesh['row'=8,'col'=4] {'row'}, use_global_device_ids=true, to_apply=%region_9.10 | all-reduce | flops 256 | bytes 2048 | tf_op jit(solution)/shard_map/psum | solution.py:125
  290.1 10.1 %all_to_all.62 = bf16[32,8,256]{2,1,0:T(8,128)(2,1)S(1)} all-to-all(bf16[32,8,256]{2,1,0:T(8,128)(2,1)S(1)} %bitcast.217), channel_id=1, replica_groups=mesh['row'=8,'col'=4] {'row','col'}, dimensions={0} | all-to-all | bytes 262144 | tf_op jit(solution)/shard_map/all_to_all | solution.py:88
  301.1 9.1 %all-gather.3 = bf16[1024,256]{1,0:T(8,128)(2,1)S(1)} all-gather(bf16[128,256]{1,0:T(8,128)(2,1)S(1)} %gather_fusion.17), channel_id=5, replica_groups=mesh['row'=8,'col'=4] {'row'}, dimensions={0}, use_global_device_ids=true | all-gather | bytes 589824 | tf_op jit(solution)/shard_map/all_gather | solution.py:97
  316.5 20.1 %reduce-scatter.13.cloned.1.call-done = f32[128,256]{0,1:T(8,128)} async-done(((f32[512,256]{0,1:T(8,128)}), f32[128,256]{0,1:T(8,128)}) %reduce-scatter.13.cloned.1.call-update) | async-done | bytes 131088 | tf_op jit(solution)/shard_map/reduce_scatter | solution.py:98
  350.3 5.2 fusion.62
  355.5 4.7 gather_fusion.19
  364.5 14.0 %all_to_all.63 = bf16[32,8,256]{2,1,0:T(8,128)(2,1)S(1)} all-to-all(bf16[32,8,256]{2,1,0:T(8,128)(2,1)S(1)} %bitcast.218), channel_id=1, replica_groups=mesh['row'=8,'col'=4] {'row','col'}, dimensions={0} | all-to-all | bytes 262144 | tf_op jit(solution)/shard_map/all_to_all | solution.py:88
  379.3 9.1 %all-gather.4 = bf16[1024,256]{1,0:T(8,128)(2,1)S(1)} all-gather(bf16[128,256]{1,0:T(8,128)(2,1)S(1)} %gather_fusion.22), channel_id=6, replica_groups=mesh['row'=8,'col'=4] {'row'}, dimensions={0}, use_global_device_ids=true | all-gather | bytes 589824 | tf_op jit(solution)/shard_map/all_gather | solution.py:97
  394.7 20.0 %reduce-scatter.15.cloned.1.call-done = f32[128,256]{0,1:T(8,128)} async-done(((f32[512,256]{0,1:T(8,128)}), f32[128,256]{0,1:T(8,128)}) %reduce-scatter.15.cloned.1.call-update) | async-done | bytes 131088 | tf_op jit(solution)/shard_map/reduce_scatter | solution.py:98
  417.4 4.7 all-to-all-start.9
  428.8 5.2 fusion.63
  443.3 14.0 %all_to_all.64 = bf16[32,8,256]{2,1,0:T(8,128)(2,1)S(1)} all-to-all(bf16[32,8,256]{2,1,0:T(8,128)(2,1)S(1)} %bitcast.214), channel_id=1, replica_groups=mesh['row'=8,'col'=4] {'row','col'}, dimensions={0} | all-to-all | bytes 262144 | tf_op jit(solution)/shard_map/all_to_all | solution.py:88
  458.1 9.1 %all-gather.5 = bf16[1024,256]{1,0:T(8,128)(2,1)S(1)} all-gather(bf16[128,256]{1,0:T(8,128)(2,1)S(1)} %gather_fusion.27), channel_id=7, replica_groups=mesh['row'=8,'col'=4] {'row'}, dimensions={0}, use_global_device_ids=true | all-gather | bytes 589824 | tf_op jit(solution)/shard_map/all_gather | solution.py:97
  472.7 21.1 %reduce-scatter.17.cloned.1.call-done = f32[128,256]{0,1:T(8,128)} async-done(((f32[512,256]{0,1:T(8,128)}), f32[128,256]{0,1:T(8,128)}) %reduce-scatter.17.cloned.1.call-update) | async-done | bytes 131088 | tf_op jit(solution)/shard_map/reduce_scatter | solution.py:98
  507.0 5.2 fusion.64
  519.3 12.0 %psum.30 = f32[256]{0:T(256)S(1)} all-reduce(f32[256]{0:T(256)S(1)} %get-tuple-element.5), channel_id=1, replica_groups=mesh['row'=8,'col'=4] {'col'}, use_global_device_ids=true, to_apply=%region_14.15 | all-reduce | flops 256 | bytes 2048 | tf_op jit(solution)/shard_map/psum | solution.py:125
  531.3 11.9 %psum.31 = f32[256]{0:T(256)S(1)} all-reduce(f32[256]{0:T(256)S(1)} %psum.30), channel_id=1, replica_groups=mesh['row'=8,'col'=4] {'row'}, use_global_device_ids=true, to_apply=%region_15.16 | all-reduce | flops 256 | bytes 2048 | tf_op jit(solution)/shard_map/psum | solution.py:125
  (161 shorter events, 178.2 us)
Async XLA Ops:
  6.5 85.4 %copy-start = (f32[8,3,128,128]{3,2,1,0:T(8,128)S(1)}, f32[8,3,128,128]{3,2,1,0:T(8,128)}, u32[]{:S(2)}) copy-start(f32[8,3,128,128]{3,2,1,0:T(8,128)} %param.8) | copy-start | bytes 4718596
  26.3 17.2 %copy-start.2 = (s32[8,3]{0,1:T(4,128)S(1)}, s32[8,3]{0,1:T(4,128)}, u32[]{:S(2)}) copy-start(s32[8,3]{0,1:T(4,128)} %param.9) | copy-start | bytes 292
  26.4 32.3 %copy-start.1 = (bf16[512,1024]{1,0:T(8,128)(2,1)S(1)}, bf16[512,1024]{1,0:T(8,128)(2,1)}, u32[]{:S(2)}) copy-start(bf16[512,1024]{1,0:T(8,128)(2,1)} %param.11) | copy-start | bytes 3145732
  28.2 15.7 %all-to-all-start = ((bf16[32,8,256]{2,1,0:T(8,128)(2,1)}), bf16[32,8,256]{2,1,0:T(8,128)(2,1)S(1)}, u32[]{:S(2)}, u32[]{:S(2)}) async-start(bf16[32,8,256]{2,1,0:T(8,128)(2,1)} %bitcast.8), calls=%async_computation | async-start | bytes 262144 | tf_op jit(solution)/shard_map/all_to_all | solution.py:88
  35.5 44.4 %reduce-scatter.7.cloned.1.call-start = ((), (), s32[]{:S(2)}) async-start(), calls=%async_computation.18 | async-start | bytes 655360 | tf_op jit(solution)/shard_map/reduce_scatter | solution.py:98
  37.5 48.1 %collective-permute-start = (f32[256,256]{1,0:T(8,128)}, f32[256,256]{1,0:T(8,128)S(1)}, u32[]{:S(2)}, u32[]{:S(2)}) collective-permute-start(f32[256,256]{1,0:T(8,128)} %get-tuple-element.31), channel_id=1, source_target_pairs={{0,1},{1,2},{2,3},{3,4},{4,5},{5,6},{6,7},{7,8},{8,9},{9,10},{10,1... | collective-permute-start | bytes 786440 | tf_op jit(solution)/shard_map/ppermute | solution.py:15
  41.1 44.4 %collective-permute-start.1 = (f32[256,256]{1,0:T(8,128)}, f32[256,256]{1,0:T(8,128)}, u32[]{:S(2)}, u32[]{:S(2)}) collective-permute-start(f32[256,256]{1,0:T(8,128)} %get-tuple-element.32), channel_id=1, source_target_pairs={{1,0},{2,1},{3,2},{4,3},{5,4},{6,5},{7,6},{8,7},{9,8},{10,9},{11,1... | collective-permute-start | bytes 786440 | tf_op jit(solution)/shard_map/ppermute | solution.py:18
  44.8 15.4 %copy-start.3 = (s32[256]{0:T(256)S(1)}, s32[256]{0:T(256)}, u32[]{:S(2)}) copy-start(s32[256]{0:T(256)} %param.13) | copy-start | bytes 3076
  44.8 15.4 %copy-start.4 = (s32[256]{0:T(256)S(1)}, s32[256]{0:T(256)}, u32[]{:S(2)}) copy-start(s32[256]{0:T(256)} %param.12) | copy-start | bytes 3076
  82.6 14.5 %all-to-all-start.1 = ((f32[32,8,256]{2,1,0:T(8,128)}), f32[32,8,256]{2,1,0:T(8,128)S(1)}, u32[]{:S(2)}, u32[]{:S(2)}) async-start(f32[32,8,256]{2,1,0:T(8,128)} %bitcast.15), calls=%async_computation.2 | async-start | bytes 524288 | tf_op jit(solution)/shard_map/all_to_all | solution.py:101
  85.5 71.3 %reduce-scatter.9.cloned.1.call-start = ((), (), s32[]{:S(2)}) async-start(), calls=%async_computation.19 | async-start | bytes 655360 | tf_op jit(solution)/shard_map/reduce_scatter | solution.py:98
  133.7 30.6 %collective-permute-start.2 = (f32[256,256]{1,0:T(8,128)}, f32[256,256]{1,0:T(8,128)S(1)}, u32[]{:S(2)}, u32[]{:S(2)}) collective-permute-start(f32[256,256]{1,0:T(8,128)} %get-tuple-element.29), channel_id=1, source_target_pairs={{0,1},{1,2},{2,3},{3,4},{4,5},{5,6},{6,7},{7,8},{8,9},{9,10},{10,1... | collective-permute-start | bytes 786440 | tf_op jit(solution)/shard_map/ppermute | solution.py:15
  135.5 28.8 %collective-permute-start.3 = (f32[256,256]{1,0:T(8,128)}, f32[256,256]{1,0:T(8,128)}, u32[]{:S(2)}, u32[]{:S(2)}) collective-permute-start(f32[256,256]{1,0:T(8,128)} %get-tuple-element.30), channel_id=1, source_target_pairs={{1,0},{2,1},{3,2},{4,3},{5,4},{6,5},{7,6},{8,7},{9,8},{10,9},{11,1... | collective-permute-start | bytes 786440 | tf_op jit(solution)/shard_map/ppermute | solution.py:18
  159.5 16.3 %all-to-all-start.3 = ((f32[32,8,256]{2,1,0:T(8,128)}), f32[32,8,256]{2,1,0:T(8,128)S(1)}, u32[]{:S(2)}, u32[]{:S(2)}) async-start(f32[32,8,256]{2,1,0:T(8,128)} %bitcast.27), calls=%async_computation.5 | async-start | bytes 524288 | tf_op jit(solution)/shard_map/all_to_all | solution.py:101
  164.2 71.3 %reduce-scatter.11.cloned.1.call-start = ((), (), s32[]{:S(2)}) async-start(), calls=%async_computation.20 | async-start | bytes 655360 | tf_op jit(solution)/shard_map/reduce_scatter | solution.py:98
  212.4 30.5 %collective-permute-start.4 = (f32[256,256]{1,0:T(8,128)}, f32[256,256]{1,0:T(8,128)S(1)}, u32[]{:S(2)}, u32[]{:S(2)}) collective-permute-start(f32[256,256]{1,0:T(8,128)} %get-tuple-element.27), channel_id=1, source_target_pairs={{0,1},{1,2},{2,3},{3,4},{4,5},{5,6},{6,7},{7,8},{8,9},{9,10},{10,1... | collective-permute-start | bytes 786440 | tf_op jit(solution)/shard_map/ppermute | solution.py:15
  214.1 28.8 %collective-permute-start.5 = (f32[256,256]{1,0:T(8,128)}, f32[256,256]{1,0:T(8,128)}, u32[]{:S(2)}, u32[]{:S(2)}) collective-permute-start(f32[256,256]{1,0:T(8,128)} %get-tuple-element.28), channel_id=1, source_target_pairs={{1,0},{2,1},{3,2},{4,3},{5,4},{6,5},{7,6},{8,7},{9,8},{10,9},{11,1... | collective-permute-start | bytes 786440 | tf_op jit(solution)/shard_map/ppermute | solution.py:18
  238.2 16.3 %all-to-all-start.5 = ((f32[32,8,256]{2,1,0:T(8,128)}), f32[32,8,256]{2,1,0:T(8,128)S(1)}, u32[]{:S(2)}, u32[]{:S(2)}) async-start(f32[32,8,256]{2,1,0:T(8,128)} %bitcast.38), calls=%async_computation.8 | async-start | bytes 524288 | tf_op jit(solution)/shard_map/all_to_all | solution.py:101
  242.9 93.7 %reduce-scatter.13.cloned.1.call-start = ((), (), s32[]{:S(2)}) async-start(), calls=%async_computation.21 | async-start | bytes 655360 | tf_op jit(solution)/shard_map/reduce_scatter | solution.py:98
  313.4 30.5 %collective-permute-start.6 = (f32[256,256]{1,0:T(8,128)}, f32[256,256]{1,0:T(8,128)S(1)}, u32[]{:S(2)}, u32[]{:S(2)}) collective-permute-start(f32[256,256]{1,0:T(8,128)} %get-tuple-element.25), channel_id=1, source_target_pairs={{0,1},{1,2},{2,3},{3,4},{4,5},{5,6},{6,7},{7,8},{8,9},{9,10},{10,1... | collective-permute-start | bytes 786440 | tf_op jit(solution)/shard_map/ppermute | solution.py:15
  315.2 28.8 %collective-permute-start.7 = (f32[256,256]{1,0:T(8,128)}, f32[256,256]{1,0:T(8,128)}, u32[]{:S(2)}, u32[]{:S(2)}) collective-permute-start(f32[256,256]{1,0:T(8,128)} %get-tuple-element.26), channel_id=1, source_target_pairs={{1,0},{2,1},{3,2},{4,3},{5,4},{6,5},{7,6},{8,7},{9,8},{10,9},{11,1... | collective-permute-start | bytes 786440 | tf_op jit(solution)/shard_map/ppermute | solution.py:18
  339.2 16.3 %all-to-all-start.7 = ((f32[32,8,256]{2,1,0:T(8,128)}), f32[32,8,256]{2,1,0:T(8,128)S(1)}, u32[]{:S(2)}, u32[]{:S(2)}) async-start(f32[32,8,256]{2,1,0:T(8,128)} %bitcast.49), calls=%async_computation.11 | async-start | bytes 524288 | tf_op jit(solution)/shard_map/all_to_all | solution.py:101
  343.9 70.9 %reduce-scatter.15.cloned.1.call-start = ((), (), s32[]{:S(2)}) async-start(), calls=%async_computation.22 | async-start | bytes 655360 | tf_op jit(solution)/shard_map/reduce_scatter | solution.py:98
  391.6 30.8 %collective-permute-start.8 = (f32[256,256]{1,0:T(8,128)}, f32[256,256]{1,0:T(8,128)S(1)}, u32[]{:S(2)}, u32[]{:S(2)}) collective-permute-start(f32[256,256]{1,0:T(8,128)} %get-tuple-element.23), channel_id=1, source_target_pairs={{0,1},{1,2},{2,3},{3,4},{4,5},{5,6},{6,7},{7,8},{8,9},{9,10},{10,1... | collective-permute-start | bytes 786440 | tf_op jit(solution)/shard_map/ppermute | solution.py:15
  393.4 29.0 %collective-permute-start.9 = (f32[256,256]{1,0:T(8,128)}, f32[256,256]{1,0:T(8,128)}, u32[]{:S(2)}, u32[]{:S(2)}) collective-permute-start(f32[256,256]{1,0:T(8,128)} %get-tuple-element.24), channel_id=1, source_target_pairs={{1,0},{2,1},{3,2},{4,3},{5,4},{6,5},{7,6},{8,7},{9,8},{10,9},{11,1... | collective-permute-start | bytes 786440 | tf_op jit(solution)/shard_map/ppermute | solution.py:18
  417.4 16.6 %all-to-all-start.9 = ((f32[32,8,256]{2,1,0:T(8,128)}), f32[32,8,256]{2,1,0:T(8,128)S(1)}, u32[]{:S(2)}, u32[]{:S(2)}) async-start(f32[32,8,256]{2,1,0:T(8,128)} %bitcast.60), calls=%async_computation.14 | async-start | bytes 524288 | tf_op jit(solution)/shard_map/all_to_all | solution.py:101
  422.1 71.7 %reduce-scatter.17.cloned.1.call-start = ((), (), s32[]{:S(2)}) async-start(), calls=%async_computation.23 | async-start | bytes 655360 | tf_op jit(solution)/shard_map/reduce_scatter | solution.py:98
  469.6 31.1 %collective-permute-start.10 = (f32[256,256]{1,0:T(8,128)S(1)}, f32[256,256]{1,0:T(8,128)S(1)}, u32[]{:S(2)}, u32[]{:S(2)}) collective-permute-start(f32[256,256]{1,0:T(8,128)S(1)} %get-tuple-element.21), channel_id=1, source_target_pairs={{0,1},{1,2},{2,3},{3,4},{4,5},{5,6},{6,7},{7,8},{8,9},{9,10},{10,1... | collective-permute-start | bytes 786440 | tf_op jit(solution)/shard_map/ppermute | solution.py:15
  471.4 29.3 %collective-permute-start.11 = (f32[256,256]{1,0:T(8,128)S(1)}, f32[256,256]{1,0:T(8,128)S(1)}, u32[]{:S(2)}, u32[]{:S(2)}) collective-permute-start(f32[256,256]{1,0:T(8,128)S(1)} %get-tuple-element.22), channel_id=1, source_target_pairs={{1,0},{2,1},{3,2},{4,3},{5,4},{6,5},{7,6},{8,7},{9,8},{10,9},{11,1... | collective-permute-start | bytes 786440 | tf_op jit(solution)/shard_map/ppermute | solution.py:18
  496.5 15.7 %all-to-all-start.11 = ((f32[32,8,256]{2,1,0:T(8,128)}), f32[32,8,256]{2,1,0:T(8,128)S(1)}, u32[]{:S(2)}, u32[]{:S(2)}) async-start(f32[32,8,256]{2,1,0:T(8,128)} %bitcast.71), calls=%async_computation.17 | async-start | bytes 524288 | tf_op jit(solution)/shard_map/all_to_all | solution.py:101
Sparse Core Ops, SparseCore 0:
  60.1 19.7 reduce-scatter.6
  131.9 24.8 reduce-scatter.8
  210.6 24.8 reduce-scatter.10
  311.6 24.8 reduce-scatter.12
  389.9 24.8 reduce-scatter.14
  468.7 25.0 reduce-scatter.16
